TPU v7x, 32 devices: a whole 2x2x4 slice. The times are simulated.
32 devices in a mesh: tensor: 4 (over z), dp: 4 (over y, x), replica: 2 (over core).
Axes of the slice: x: 2, y: 2, z: 4, core: 2. Of those that a mesh axis runs over, the one named last changes fastest.
Arguments:
- states: bfloat16 [8, 256, 4096], P(('dp', 'replica')), may hold values from -6 to 6
- norm_gain: float32 [4096], replicated, may hold values from 0.26 to 4.4
- gate_up: bfloat16 [4096, 2, 14336], P('replica', None, 'tensor'), may hold values from -0.09375 to 0.09375
- cotangent: bfloat16 [8, 256, 14336], P(('dp', 'replica'), None, 'tensor'), may hold values from -120 to 120
- prompt: bfloat16 [32, 4096], replicated, may hold values from -6 to 6
- step_sizes: float32 [3], replicated, may hold values from 0.3 to 1
- insert_at: int32 [8], P(('dp', 'replica')), may hold values from 0 to 224, as said below
- lengths: int32 [8], P(('dp', 'replica')), may hold values from 128 to 256, as said below
Outputs:
- prompt_final: float32 [32, 4096], P(None, 'tensor')
- weight_step: bfloat16 [4096, 2, 14336], P(('dp', 'replica'), None, 'tensor')
Inputs may be any that keep to these rules, and one draw needn't show every extreme that they name: Each prompt lies inside its sequence: insert_at[b] + 32 <= lengths[b]; in every draw some prompt begins at row 0 and some prompt ends at the last row 255. `lengths`: in every draw some sequence has all 256 rows live and some has 128.
All inputs are finite; a program needn't handle non-finite values.
Results may differ from a plain program's by a relative error of at most 0.012.
Values may be sent and summed in bfloat16 or wider, within the bound.
A program may use at most 320 MiB of HBM per device.

v0:
```python
import jax
import jax.numpy as jnp
from jax import lax
from jax.sharding import PartitionSpec as P

D = 4096
FF = 14336


def row_scale(feature_rows):
    return lax.rsqrt(jnp.mean(feature_rows * feature_rows, axis=-1, keepdims=True) + 1e-05)


def silu_parts(gate_values):
    sigmoid_value = jax.nn.sigmoid(gate_values)
    return (
        gate_values * sigmoid_value,
        sigmoid_value * (1.0 + gate_values * (1.0 - sigmoid_value)),
    )


def hidden_grads(normalized, weight_pair, cotan_rows):
    unit_count = weight_pair.shape[1] // 2
    projected = jnp.dot(normalized, weight_pair, preferred_element_type=jnp.float32)
    activated, derivative = silu_parts(projected[:, :unit_count])
    up_part = projected[:, unit_count:]
    return jnp.concatenate(
        [cotan_rows * up_part * derivative, cotan_rows * activated], axis=1
    ).astype(jnp.bfloat16)


def norm_back(shifted, inverse_rms, norm_gain, feature_grad):
    feature_mean = jnp.mean(shifted * norm_gain * feature_grad, axis=-1, keepdims=True)
    return (
        inverse_rms * norm_gain * feature_grad
        - shifted * (inverse_rms * inverse_rms * inverse_rms) * feature_mean
    )


def per_device(states, norm_gain, gate_up, cotangent, prompt, step_sizes, insert_at, lengths):
    gathered = lax.all_gather(gate_up, "replica", axis=0, tiled=True)
    feature_count = gathered.shape[0]
    unit_count = gathered.shape[2]
    weight_pair = gathered.reshape(feature_count, 2 * unit_count)
    seq_states = states[0]
    seq_cotan = cotangent[0].astype(jnp.float32)
    prompt_start = insert_at[0]
    seq_length = lengths[0]
    prompt_count = prompt.shape[0]
    prompt_base = lax.dynamic_slice_in_dim(seq_states, prompt_start, prompt_count, 0).astype(
        jnp.float32
    )
    prompt_cotan = lax.dynamic_slice_in_dim(seq_cotan, prompt_start, prompt_count, 0)
    adversary = prompt.astype(jnp.float32)
    for attack_step in range(step_sizes.shape[0]):
        shifted = prompt_base + adversary
        inverse_rms = row_scale(shifted)
        normalized = (shifted * inverse_rms * norm_gain).astype(jnp.bfloat16)
        unit_grads = hidden_grads(normalized, weight_pair, prompt_cotan)
        feature_grad = lax.dot_general(
            unit_grads, weight_pair, (((1,), (1,)), ((), ())), preferred_element_type=jnp.float32
        )
        feature_grad = lax.psum(feature_grad, "tensor")
        summed_grad = lax.psum(
            norm_back(shifted, inverse_rms, norm_gain, feature_grad), ("dp", "replica")
        )
        adversary = adversary + step_sizes[attack_step] * summed_grad * lax.rsqrt(
            jnp.mean(summed_grad * summed_grad, axis=-1, keepdims=True) + 1e-06
        )
    full_rows = lax.dynamic_update_slice_in_dim(
        seq_states.astype(jnp.float32), prompt_base + adversary, prompt_start, 0
    )
    full_normed = (full_rows * row_scale(full_rows) * norm_gain).astype(jnp.bfloat16)
    positions = lax.broadcasted_iota(jnp.int32, (full_rows.shape[0], 1), 0)
    live_cotan = jnp.where(positions < seq_length, seq_cotan, 0.0)
    token_grads = hidden_grads(full_normed, weight_pair, live_cotan)
    received = lax.all_to_all(
        full_normed, ("dp", "replica"), split_axis=1, concat_axis=0, tiled=True
    )
    weight_grad = lax.dot_general(
        received,
        lax.all_gather(token_grads, ("dp", "replica"), axis=0, tiled=True),
        (((0,), (0,)), ((), ())),
        preferred_element_type=jnp.float32,
    )
    squares = lax.psum(jnp.sum(weight_grad * weight_grad), ("tensor", "dp", "replica"))
    weight_step = (weight_grad * lax.rsqrt(squares / (2 * D * FF) + 1e-06)).astype(jnp.bfloat16)
    weight_step = weight_step.reshape(weight_grad.shape[0], 2, unit_count)
    column_count = adversary.shape[1] // lax.axis_size("tensor")
    prompt_final = lax.dynamic_slice_in_dim(
        adversary, lax.axis_index("tensor") * column_count, column_count, 1
    )
    return (prompt_final, weight_step)


def solution(mesh):
    return jax.shard_map(
        per_device,
        mesh=mesh,
        in_specs=(
            P(("dp", "replica"), None, None),
            P(),
            P("replica", None, "tensor"),
            P(("dp", "replica"), None, "tensor"),
            P(),
            P(),
            P(("dp", "replica")),
            P(("dp", "replica")),
        ),
        out_specs=(P(None, "tensor"), P(("dp", "replica"), None, "tensor")),
        check_vma=False,
    )
```

profile of v0, /device:TPU:0, one launch (start us, length us, event | category | flops | bytes accessed | tf_op | source)
XLA Modules:
  0.0 889.3 jit_solution(5123396470353676943)
XLA Ops:
  8.8 3.8 convert_element_type.43
  12.8 83.6 %all-gather.3.cloned.1.call-done = bf16[4096,2,3584]{2,1,0:T(2,128)(2,1)} async-done(((bf16[2048,2,3584]{2,1,0:T(2,128)(2,1)}), bf16[4096,2,3584]{2,1,0:T(2,128)(2,1)}) %all-gather.3.cloned.1.call-update) | async-done | bytes 58720272 | tf_op jit(solution)/shard_map/all_gather | solution.py:41
  96.4 39.3 %copy.16 = bf16[512,8,2,3584]{3,1,2,0:T(8,128)(2,1)} copy(bf16[512,8,2,3584]{3,2,1,0:T(2,128)(2,1)} %bitcast.75) | data formatting | bytes 117440512
  135.7 21.5 %fusion.23 = f32[32,7168]{1,0:T(8,128)S(1)} fusion(bf16[4096,7168]{1,0:T(8,128)(2,1)} %bitcast.68, bf16[32,4096]{1,0:T(8,128)(2,1)S(1)} %copy-done.2, f32[4096]{0:T(1024)S(1)} %copy-done.5, f32[32]{0:T(128)S(1)} %get-tuple-element.24, bf16[1,256,4096]{2,1,0:T(8,128)(2,1)S(1)} %copy-done.1, s32[]{:T(128)S(6)} %select_n.12), kind=kOutput, calls=%fused_computation.64 | convolution fusion | flops 1879834624 | bytes 60178948 | tf_op jit(solution)/shard_map/dot_general | solution.py:24
  158.5 24.7 %fusion.8 = f32[32,4096]{1,0:T(8,128)} fusion(bf16[4096,7168]{1,0:T(8,128)(2,1)} %bitcast.69, bf16[32,3584]{1,0:T(8,128)(2,1)S(1)} %get-tuple-element.15, bf16[32,3584]{1,0:T(8,128)(2,1)S(1)} %get-tuple-element.14), kind=kOutput, calls=%fused_computation.43 | convolution fusion | flops 1879965696 | bytes 59703296 | tf_op jit(solution)/shard_map/dot_general | solution.py:60
  183.3 39.6 %all-reduce.7.cloned.1.call-done = f32[32,4096]{1,0:T(8,128)} async-done(((f32[32,4096]{1,0:T(8,128)}), f32[32,4096]{1,0:T(8,128)}) %all-reduce.7.cloned.1.call-update) | async-done | bytes 524304 | tf_op jit(solution)/shard_map/psum | solution.py:63
  226.9 54.0 %all-reduce.9.cloned.1.call-done = f32[32,4096]{1,0:T(8,128)} async-done(((f32[32,4096]{1,0:T(8,128)}), f32[32,4096]{1,0:T(8,128)}) %all-reduce.9.cloned.1.call-update) | async-done | bytes 524304 | tf_op jit(solution)/shard_map/psum | solution.py:64
  284.0 21.5 %fusion.24 = f32[32,7168]{1,0:T(8,128)S(1)} fusion(bf16[4096,7168]{1,0:T(8,128)(2,1)} %bitcast.70, f32[32,4096]{1,0:T(8,128)S(1)} %get-tuple-element.7, f32[32]{0:T(128)S(1)} %get-tuple-element.22, f32[4096]{0:T(1024)S(1)} %copy-done.5), kind=kOutput, calls=%fused_computation.65 | convolution fusion | flops 1879441408 | bytes 60178560 | tf_op jit(solution)/shard_map/dot_general | solution.py:24
  306.9 24.7 %fusion.12 = f32[32,4096]{1,0:T(8,128)} fusion(bf16[4096,7168]{1,0:T(8,128)(2,1)} %bitcast.71, bf16[32,3584]{1,0:T(8,128)(2,1)S(1)} %get-tuple-element.13, bf16[32,3584]{1,0:T(8,128)(2,1)S(1)} %get-tuple-element.12), kind=kOutput, calls=%fused_computation.47 | convolution fusion | flops 1879965696 | bytes 59703296 | tf_op jit(solution)/shard_map/dot_general | solution.py:60
  331.6 37.7 %all-reduce.11.cloned.1.call-done = f32[32,4096]{1,0:T(8,128)} async-done(((f32[32,4096]{1,0:T(8,128)}), f32[32,4096]{1,0:T(8,128)}) %all-reduce.11.cloned.1.call-update) | async-done | bytes 524304 | tf_op jit(solution)/shard_map/psum | solution.py:63
  372.9 54.4 %all-reduce.13.cloned.1.call-done = f32[32,4096]{1,0:T(8,128)} async-done(((f32[32,4096]{1,0:T(8,128)}), f32[32,4096]{1,0:T(8,128)}) %all-reduce.13.cloned.1.call-update) | async-done | bytes 524304 | tf_op jit(solution)/shard_map/psum | solution.py:64
  428.5 2.6 multiply_reduce_fusion.4
  431.1 21.4 %fusion.25 = f32[32,7168]{1,0:T(8,128)S(1)} fusion(bf16[4096,7168]{1,0:T(8,128)(2,1)} %bitcast.72, f32[32]{0:T(128)S(1)} %get-tuple-element.20, f32[4096]{0:T(1024)S(1)} %copy-done.5, f32[32,4096]{1,0:T(8,128)S(1)} %get-tuple-element.5, bf16[1,256,4096]{2,1,0:T(8,128)(2,1)S(1)} %copy-done.1, s32[]{:T(128)S(6)} %select_n.12), kind=kOutput, calls=%fused_computation.66 | convolution fusion | flops 1879703552 | bytes 60441092 | tf_op jit(solution)/shard_map/dot_general | solution.py:24
  453.8 24.7 %fusion.16 = f32[32,4096]{1,0:T(8,128)} fusion(bf16[4096,7168]{1,0:T(8,128)(2,1)} %bitcast.73, bf16[32,3584]{1,0:T(8,128)(2,1)S(1)} %get-tuple-element.11, bf16[32,3584]{1,0:T(8,128)(2,1)S(1)} %get-tuple-element.10), kind=kOutput, calls=%fused_computation.51 | convolution fusion | flops 1879965696 | bytes 59703296 | tf_op jit(solution)/shard_map/dot_general | solution.py:60
  478.6 2.5 copy.13
  481.1 35.2 %all-reduce.15.cloned.1.call-done = f32[32,4096]{1,0:T(8,128)} async-done(((f32[32,4096]{1,0:T(8,128)}), f32[32,4096]{1,0:T(8,128)}) %all-reduce.15.cloned.1.call-update) | async-done | bytes 524304 | tf_op jit(solution)/shard_map/psum | solution.py:63
  520.2 3.9 bitcast_convert_fusion
  524.8 49.5 %all-reduce.17.cloned.1.call-done = f32[32,4096]{1,0:T(8,128)} async-done(((f32[32,4096]{1,0:T(8,128)}), f32[32,4096]{1,0:T(8,128)}) %all-reduce.17.cloned.1.call-update) | async-done | bytes 524304 | tf_op jit(solution)/shard_map/psum | solution.py:64
  575.5 2.7 convert_add_fusion
  578.8 11.9 %dynamic_update_slice.3 = f32[256,4096]{0,1:T(8,128)} dynamic-update-slice(f32[256,4096]{0,1:T(8,128)} %bitcast_convert_fusion, f32[32,4096]{0,1:T(8,128)S(1)} %copy.14, s32[]{:T(128)S(6)} %select_n.12, s32[]{:T(128)} %constant.15.clone.1) | dynamic-update-slice | bytes 1048580 | tf_op jit(solution)/shard_map/dynamic_update_slice | solution.py:70
  590.7 2.9 multiply_reduce_fusion.1
  595.9 28.3 %fusion.39 = f32[256,7168]{1,0:T(8,128)} fusion(bf16[256,4096]{0,1:T(8,128)(2,1)} %multiply_convert_fusion.1, bf16[4096,7168]{1,0:T(8,128)(2,1)} %bitcast.74), kind=kOutput, calls=%fused_computation.95 | convolution fusion | flops 15032385536 | bytes 68157440 | tf_op jit(solution)/shard_map/dot_general | solution.py:24
  624.2 4.1 fusion.1
  628.3 2.3 pad_maximum_fusion
  630.6 3.8 all-to-all-start
  636.0 41.6 %all-to-all-done = bf16[256,8,512]{0,2,1:T(8,128)(2,1)S(1)} async-done(((bf16[256,8,512]{0,2,1:T(8,128)(2,1)}), bf16[256,8,512]{0,2,1:T(8,128)(2,1)S(1)}, u32[]{:S(2)}, u32[]{:S(2)}) %all-to-all-start) | async-done | bytes 2097184 | tf_op jit(solution)/shard_map/all_to_all | solution.py:77
  677.6 2.4 copy.15
  680.0 109.1 %all-gather.5.cloned.1.call-done = bf16[2048,7168]{1,0:T(8,128)(2,1)} async-done(((bf16[256,7168]{1,0:T(8,128)(2,1)}), bf16[2048,7168]{1,0:T(8,128)(2,1)}) %all-gather.5.cloned.1.call-update) | async-done | bytes 29360144 | tf_op jit(solution)/shard_map/all_gather | solution.py:82
  789.1 26.1 %multiply_reduce_fusion = (f32[]{:T(128)}, f32[512,7168]{1,0:T(8,128)}) fusion(bf16[2048,512]{1,0:T(8,128)(2,1)} %bitcast.77, bf16[2048,7168]{1,0:T(8,128)(2,1)} %all-gather.5.cloned.1.call-done), kind=kOutput, calls=%fused_computation.1 | convolution fusion | flops 15039725568 | bytes 46137348 | tf_op jit(solution)/shard_map/dot_general | solution.py:80
  815.2 39.7 %psum.55 = f32[]{:T(128)} all-reduce(f32[]{:T(128)} %get-tuple-element.25), channel_id=1, replica_groups=mesh['tensor'=4,'dp'=4,'replica'=2] {'tensor','dp','replica'}, use_global_device_ids=true, to_apply=%region_17.18 | all-reduce | flops 1 | bytes 8 | tf_op jit(solution)/shard_map/psum | solution.py:86
  855.6 9.8 %multiply_convert_fusion = bf16[512,7168]{1,0:T(8,128)(2,1)} fusion(f32[512,7168]{1,0:T(8,128)} %get-tuple-element.26, f32[]{:T(128)S(6)} %rsqrt.75), kind=kLoop, calls=%fused_computation | loop fusion | flops 7340032 | bytes 22020100 | tf_op jit(solution)/shard_map/convert_element_type | solution.py:87
  865.4 16.9 %reshape.113 = bf16[512,2,3584]{2,1,0:T(2,128)(2,1)} reshape(bf16[512,7168]{1,0:T(8,128)(2,1)} %multiply_convert_fusion) | data formatting | bytes 14680064 | tf_op jit(solution)/shard_map/reshape | solution.py:88
  (59 shorter events, 26.6 us)
Async XLA Ops:
  7.2 89.3 %all-gather.3.cloned.1.call-start = ((), (), s32[]{:S(2)}) async-start(), calls=%async_computation.1 | async-start | bytes 88080384 | tf_op jit(solution)/shard_map/all_gather | solution.py:41
  7.9 4.6 copy-start.1
  7.9 4.6 copy-start.2
  7.9 214.9 %all-reduce.7.cloned.1.call-start = ((), (), s32[]{:S(2)}) async-start(), calls=%async_computation.2 | async-start | bytes 1048576 | tf_op jit(solution)/shard_map/psum | solution.py:63
  96.4 39.3 %copy-start.5 = (f32[4096]{0:T(1024)S(1)}, f32[4096]{0:T(1024)}, u32[]{:S(2)}) copy-start(f32[4096]{0:T(1024)} %param.9) | copy-start | bytes 49156
  183.2 43.0 %copy-start.6 = (f32[3]{0:T(128)S(1)}, f32[3]{0:T(128)}, u32[]{:S(2)}) copy-start(f32[3]{0:T(128)} %param.13) | copy-start | bytes 40
  183.3 97.6 %all-reduce.9.cloned.1.call-start = ((), (), s32[]{:S(2)}) async-start(), calls=%async_computation.3 | async-start | bytes 1048576 | tf_op jit(solution)/shard_map/psum | solution.py:64
  226.2 143.1 %all-reduce.11.cloned.1.call-start = ((), (), s32[]{:S(2)}) async-start(), calls=%async_computation.4 | async-start | bytes 1048576 | tf_op jit(solution)/shard_map/psum | solution.py:63
  331.5 96.9 %copy-start.4 = (f32[32,4096]{1,0:T(8,128)S(1)}, f32[32,4096]{1,0:T(8,128)}, u32[]{:S(2)}) copy-start(f32[32,4096]{1,0:T(8,128)} %all-reduce.9.cloned.1.call-done) | copy-start | bytes 1572868
  331.6 95.7 %all-reduce.13.cloned.1.call-start = ((), (), s32[]{:S(2)}) async-start(), calls=%async_computation.5 | async-start | bytes 1048576 | tf_op jit(solution)/shard_map/psum | solution.py:64
  372.6 143.8 %all-reduce.15.cloned.1.call-start = ((), (), s32[]{:S(2)}) async-start(), calls=%async_computation.6 | async-start | bytes 1048576 | tf_op jit(solution)/shard_map/psum | solution.py:63
  478.6 95.8 %all-reduce.17.cloned.1.call-start = ((), (), s32[]{:S(2)}) async-start(), calls=%async_computation.7 | async-start | bytes 1048576 | tf_op jit(solution)/shard_map/psum | solution.py:64
  519.6 269.4 %all-gather.5.cloned.1.call-start = ((), (), s32[]{:S(2)}) async-start(), calls=%async_computation.8 | async-start | bytes 33030144 | tf_op jit(solution)/shard_map/all_gather | solution.py:82
  590.7 3.4 copy-start
  595.9 28.3 %copy-start.3 = (bf16[1,256,3584]{2,1,0:T(8,128)(2,1)S(1)}, bf16[1,256,3584]{2,1,0:T(8,128)(2,1)}, u32[]{:S(2)}) copy-start(bf16[1,256,3584]{2,1,0:T(8,128)(2,1)} %param.11) | copy-start | bytes 5505028
  630.6 47.0 %all-to-all-start = ((bf16[256,8,512]{0,2,1:T(8,128)(2,1)}), bf16[256,8,512]{0,2,1:T(8,128)(2,1)S(1)}, u32[]{:S(2)}, u32[]{:S(2)}) async-start(bf16[256,8,512]{0,2,1:T(8,128)(2,1)} %bitcast.8), calls=%async_computation | async-start | bytes 4194304 | tf_op jit(solution)/shard_map/all_to_all | solution.py:77
Sparse Core Ops, SparseCore 0:
  9.5 86.8 all-gather.2
  183.4 39.4 all-reduce.6
  226.3 54.5 all-reduce.8
  331.7 37.5 all-reduce.10
  372.7 54.5 all-reduce.12
  478.7 37.5 all-reduce.14
  519.8 54.5 all-reduce.16
  630.7 158.2 all-gather.4
where the time goes:
time: 900 us; the launch traced here: 889 us
  waiting for transfers between devices  505 us (56%)
  matrix products  193 us (21%)
  local copies, waits for them, and re-layouts  76.3 us (8%)
  other arithmetic  53.3 us (6%)
  blocking collectives  39.7 us (4%)
  between operations  16.6 us (2%)
    psum x3, waiting for transfers between devices, per_device(): lax.psum(norm_back(shifted, inverse_rms, norm_gain, feature_grad), ('dp',...  158 us
    psum x3, waiting for transfers between devices, per_device(): feature_grad = lax.psum(feature_grad, 'tensor')  112 us
    all_gather x1, waiting for transfers between devices, per_device(): lax.all_gather(token_grads, ('dp', 'replica'), axis=0, tiled=True)  109 us
    dot_general x4, matrix products, hidden_grads(): jnp.dot(normalized, weight_pair, preferred_element_type=jnp.float32)  92.8 us
    all_gather x1, waiting for transfers between devices, per_device(): gathered = lax.all_gather(gate_up, 'replica', axis=0, tiled=True)  83.6 us
    dot_general x3, matrix products, per_device(): lax.dot_general(unit_grads, weight_pair, (((1,), (1,)), ((), ())), prefer...  74.1 us
    unnamed x16, local copies, waits for them, and re-layouts  42.3 us
    all_to_all x1, waiting for transfers between devices, per_device(): lax.all_to_all(full_normed, ('dp', 'replica'), split_axis=1, concat_axis=...  41.6 us
  transfers between devices with their start and end apart: 9, of which 9 were waited for; matrix products, arithmetic and copies ran while one was open for 2% of the time, Pallas kernels for 0%

commit v1 on v0

--- a/solution.py
+++ b/solution.py
@@ -74,9 +74,20 @@
     positions = lax.broadcasted_iota(jnp.int32, (full_rows.shape[0], 1), 0)
     live_cotan = jnp.where(positions < seq_length, seq_cotan, 0.0)
     token_grads = hidden_grads(full_normed, weight_pair, live_cotan)
-    received = lax.all_to_all(
-        full_normed, ("dp", "replica"), split_axis=1, concat_axis=0, tiled=True
-    )
+    heard, tall = (jax.lax.axis_size(("dp", "replica")), jax.lax.axis_index(("dp", "replica")))
+    e_now = full_normed.shape[1] // heard
+    res = list(full_normed.shape)
+    res[1] = e_now
+    local_out = res[0]
+    res[0] = local_out * heard
+    received = jnp.zeros(res, full_normed.dtype)
+    for to_i in range(heard):
+        w2 = lax.dynamic_slice_in_dim(full_normed, (tall ^ to_i) * e_now, e_now, axis=1)
+        if to_i:
+            w2 = jax.lax.ppermute(
+                w2, axis_name=("dp", "replica"), perm=[(d, d ^ to_i) for d in range(heard)]
+            )
+        received = lax.dynamic_update_slice_in_dim(received, w2, (tall ^ to_i) * local_out, axis=0)
     weight_grad = lax.dot_general(
         received,
         lax.all_gather(token_grads, ("dp", "replica"), axis=0, tiled=True),

time: 900 us -> 886 us (0.984)
    all_to_all x1 -> x0, waiting for transfers between devices: 41.6 us -> none  [per_device(): lax.all_to_all(full_normed, ('dp', 'replica'), split_axis=1, concat_axis=...]
    ppermute x0 -> x7, waiting for transfers between devices: none -> 30 us  [per_device(): jax.lax.ppermute(w2, axis_name=('dp', 'replica'), perm=[(d, d ^ to_i) for...]
    dynamic_update_slice x1, local copies, waits for them, and re-layouts: 11.9 us -> 2.91 us  [per_device(): lax.dynamic_update_slice_in_dim(seq_states.astype(jnp.float32), prompt_ba...]
    unnamed x16 -> x15, local copies, waits for them, and re-layouts: 42.3 us -> 41.3 us
  transfers between devices with their start and end apart: 9 -> 15, of which waited for: 9 -> 13; matrix products, arithmetic and copies ran while one was open for 2% -> 2% of each run, Pallas kernels for 0% -> 0%
where the time goes in v1:
time: 886 us; the launch traced here: 876 us
  waiting for transfers between devices  504 us (57%)
  matrix products  191 us (22%)
  local copies, waits for them, and re-layouts  69.5 us (8%)
  other arithmetic  51 us (6%)
  blocking collectives  39.7 us (4%)
  between operations  16.7 us (2%)
    psum x3, waiting for transfers between devices, per_device(): lax.psum(norm_back(shifted, inverse_rms, norm_gain, feature_grad), ('dp',...  160 us
    psum x3, waiting for transfers between devices, per_device(): feature_grad = lax.psum(feature_grad, 'tensor')  115 us
    all_gather x1, waiting for transfers between devices, per_device(): lax.all_gather(token_grads, ('dp', 'replica'), axis=0, tiled=True)  115 us
    dot_general x4, matrix products, hidden_grads(): jnp.dot(normalized, weight_pair, preferred_element_type=jnp.float32)  90.3 us
    all_gather x1, waiting for transfers between devices, per_device(): gathered = lax.all_gather(gate_up, 'replica', axis=0, tiled=True)  83.6 us
    dot_general x3, matrix products, per_device(): lax.dot_general(unit_grads, weight_pair, (((1,), (1,)), ((), ())), prefer...  74.1 us
    unnamed x15, local copies, waits for them, and re-layouts  41.3 us
    psum x1, blocking collectives, per_device(): lax.psum(jnp.sum(weight_grad * weight_grad), ('tensor', 'dp', 'replica'))  39.7 us
  transfers between devices with their start and end apart: 15, of which 13 were waited for; matrix products, arithmetic and copies ran while one was open for 2% of the time, Pallas kernels for 0%

profile of v1, /device:TPU:0, one launch (start us, length us, event | category | flops | bytes accessed | tf_op | source)
XLA Modules:
  0.0 876.4 jit_solution(4359876409488670402)
XLA Ops:
  8.8 3.8 convert_element_type.43
  12.8 83.6 %all-gather.3.cloned.1.call-done = bf16[4096,2,3584]{2,1,0:T(2,128)(2,1)} async-done(((bf16[2048,2,3584]{2,1,0:T(2,128)(2,1)}), bf16[4096,2,3584]{2,1,0:T(2,128)(2,1)}) %all-gather.3.cloned.1.call-update) | async-done | bytes 58720272 | tf_op jit(solution)/shard_map/all_gather | solution.py:41
  96.4 39.3 %copy.10 = bf16[512,8,2,3584]{3,1,2,0:T(8,128)(2,1)} copy(bf16[512,8,2,3584]{3,2,1,0:T(2,128)(2,1)} %bitcast.72) | data formatting | bytes 117440512
  135.7 21.5 %fusion.23 = f32[32,7168]{1,0:T(8,128)S(1)} fusion(bf16[4096,7168]{1,0:T(8,128)(2,1)} %bitcast.65, bf16[32,4096]{1,0:T(8,128)(2,1)S(1)} %copy-done.2, f32[4096]{0:T(1024)S(1)} %copy-done.4, f32[32]{0:T(128)S(1)} %get-tuple-element.32, bf16[1,256,4096]{2,1,0:T(8,128)(2,1)S(1)} %copy-done.1, s32[]{:T(128)S(6)} %select_n.60), kind=kOutput, calls=%fused_computation.64 | convolution fusion | flops 1879834624 | bytes 60178948 | tf_op jit(solution)/shard_map/dot_general | solution.py:24
  158.5 24.7 %fusion.8 = f32[32,4096]{1,0:T(8,128)} fusion(bf16[4096,7168]{1,0:T(8,128)(2,1)} %bitcast.66, bf16[32,3584]{1,0:T(8,128)(2,1)S(1)} %get-tuple-element.15, bf16[32,3584]{1,0:T(8,128)(2,1)S(1)} %get-tuple-element.14), kind=kOutput, calls=%fused_computation.43 | convolution fusion | flops 1879965696 | bytes 59703296 | tf_op jit(solution)/shard_map/dot_general | solution.py:60
  183.3 39.6 %all-reduce.7.cloned.1.call-done = f32[32,4096]{1,0:T(8,128)} async-done(((f32[32,4096]{1,0:T(8,128)}), f32[32,4096]{1,0:T(8,128)}) %all-reduce.7.cloned.1.call-update) | async-done | bytes 524304 | tf_op jit(solution)/shard_map/psum | solution.py:63
  226.9 54.0 %all-reduce.9.cloned.1.call-done = f32[32,4096]{1,0:T(8,128)} async-done(((f32[32,4096]{1,0:T(8,128)}), f32[32,4096]{1,0:T(8,128)}) %all-reduce.9.cloned.1.call-update) | async-done | bytes 524304 | tf_op jit(solution)/shard_map/psum | solution.py:64
  284.0 21.5 %fusion.24 = f32[32,7168]{1,0:T(8,128)S(1)} fusion(bf16[4096,7168]{1,0:T(8,128)(2,1)} %bitcast.67, f32[32,4096]{1,0:T(8,128)S(1)} %get-tuple-element.7, f32[32]{0:T(128)S(1)} %get-tuple-element.30, f32[4096]{0:T(1024)S(1)} %copy-done.4), kind=kOutput, calls=%fused_computation.65 | convolution fusion | flops 1879441408 | bytes 60178560 | tf_op jit(solution)/shard_map/dot_general | solution.py:24
  306.9 24.7 %fusion.12 = f32[32,4096]{1,0:T(8,128)} fusion(bf16[4096,7168]{1,0:T(8,128)(2,1)} %bitcast.68, bf16[32,3584]{1,0:T(8,128)(2,1)S(1)} %get-tuple-element.13, bf16[32,3584]{1,0:T(8,128)(2,1)S(1)} %get-tuple-element.12), kind=kOutput, calls=%fused_computation.47 | convolution fusion | flops 1879965696 | bytes 59703296 | tf_op jit(solution)/shard_map/dot_general | solution.py:60
  331.6 37.7 %all-reduce.11.cloned.1.call-done = f32[32,4096]{1,0:T(8,128)} async-done(((f32[32,4096]{1,0:T(8,128)}), f32[32,4096]{1,0:T(8,128)}) %all-reduce.11.cloned.1.call-update) | async-done | bytes 524304 | tf_op jit(solution)/shard_map/psum | solution.py:63
  373.1 54.2 %all-reduce.13.cloned.1.call-done = f32[32,4096]{1,0:T(8,128)} async-done(((f32[32,4096]{1,0:T(8,128)}), f32[32,4096]{1,0:T(8,128)}) %all-reduce.13.cloned.1.call-update) | async-done | bytes 524304 | tf_op jit(solution)/shard_map/psum | solution.py:64
  428.5 2.6 multiply_reduce_fusion.4
  431.1 21.4 %fusion.25 = f32[32,7168]{1,0:T(8,128)S(1)} fusion(bf16[4096,7168]{1,0:T(8,128)(2,1)} %bitcast.69, f32[32]{0:T(128)S(1)} %get-tuple-element.28, f32[4096]{0:T(1024)S(1)} %copy-done.4, f32[32,4096]{1,0:T(8,128)S(1)} %get-tuple-element.5, bf16[1,256,4096]{2,1,0:T(8,128)(2,1)S(1)} %copy-done.1, s32[]{:T(128)S(6)} %select_n.60), kind=kOutput, calls=%fused_computation.66 | convolution fusion | flops 1879703552 | bytes 60441092 | tf_op jit(solution)/shard_map/dot_general | solution.py:24
  453.8 24.7 %fusion.16 = f32[32,4096]{1,0:T(8,128)} fusion(bf16[4096,7168]{1,0:T(8,128)(2,1)} %bitcast.70, bf16[32,3584]{1,0:T(8,128)(2,1)S(1)} %get-tuple-element.11, bf16[32,3584]{1,0:T(8,128)(2,1)S(1)} %get-tuple-element.10), kind=kOutput, calls=%fused_computation.51 | convolution fusion | flops 1879965696 | bytes 59703296 | tf_op jit(solution)/shard_map/dot_general | solution.py:60
  478.6 37.7 %all-reduce.15.cloned.1.call-done = f32[32,4096]{1,0:T(8,128)} async-done(((f32[32,4096]{1,0:T(8,128)}), f32[32,4096]{1,0:T(8,128)}) %all-reduce.15.cloned.1.call-update) | async-done | bytes 524304 | tf_op jit(solution)/shard_map/psum | solution.py:63
  519.7 2.5 bitcast_convert_fusion
  522.9 51.5 %all-reduce.17.cloned.1.call-done = f32[32,4096]{1,0:T(8,128)} async-done(((f32[32,4096]{1,0:T(8,128)}), f32[32,4096]{1,0:T(8,128)}) %all-reduce.17.cloned.1.call-update) | async-done | bytes 524304 | tf_op jit(solution)/shard_map/psum | solution.py:64
  575.5 2.7 convert_add_fusion
  578.2 2.9 dynamic_update_slice.27
  581.1 2.7 multiply_reduce_fusion.1
  585.1 25.9 %fusion.39 = f32[256,7168]{1,0:T(8,128)} fusion(bf16[256,4096]{1,0:T(8,128)(2,1)S(1)} %multiply_convert_fusion.1, bf16[4096,7168]{1,0:T(8,128)(2,1)} %bitcast.71), kind=kOutput, calls=%fused_computation.110 | convolution fusion | flops 15032385536 | bytes 68157440 | tf_op jit(solution)/shard_map/dot_general | solution.py:24
  611.0 4.6 fusion.1
  626.9 2.8 collective-permute-done.1
  630.4 7.9 collective-permute-done.2
  639.8 2.6 collective-permute-done.4
  643.1 7.1 collective-permute-done.5
  651.0 9.5 %collective-permute-done.6 = bf16[256,512]{1,0:T(8,128)(2,1)S(1)} collective-permute-done((bf16[256,512]{1,0:T(8,128)(2,1)S(1)}, bf16[256,512]{1,0:T(8,128)(2,1)S(1)}, u32[]{:S(2)}, u32[]{:S(2)}) %collective-permute-start.6) | collective-permute-done | bytes 262176 | tf_op jit(solution)/shard_map/ppermute | solution.py:87
  661.2 114.8 %all-gather.5.cloned.1.call-done = bf16[2048,7168]{1,0:T(8,128)(2,1)} async-done(((bf16[256,7168]{1,0:T(8,128)(2,1)}), bf16[2048,7168]{1,0:T(8,128)(2,1)}) %all-gather.5.cloned.1.call-update) | async-done | bytes 29360144 | tf_op jit(solution)/shard_map/all_gather | solution.py:93
  775.9 26.3 %multiply_reduce_fusion = (f32[]{:T(128)}, f32[512,7168]{1,0:T(8,128)}) fusion(bf16[2048,512]{1,0:T(8,128)(2,1)} %constant_dynamic-update-slice_fusion, bf16[2048,7168]{1,0:T(8,128)(2,1)} %all-gather.5.cloned.1.call-done), kind=kOutput, calls=%fused_computation.1 | convolution fusion | flops 15039725568 | bytes 46137348 | tf_op jit(solution)/shard_map/dot_general | solution.py:91
  802.3 39.7 %psum.55 = f32[]{:T(128)} all-reduce(f32[]{:T(128)} %get-tuple-element.33), channel_id=1, replica_groups=mesh['tensor'=4,'dp'=4,'replica'=2] {'tensor','dp','replica'}, use_global_device_ids=true, to_apply=%region_17.18 | all-reduce | flops 1 | bytes 8 | tf_op jit(solution)/shard_map/psum | solution.py:97
  842.7 9.8 %multiply_convert_fusion = bf16[512,7168]{1,0:T(8,128)(2,1)} fusion(f32[512,7168]{1,0:T(8,128)} %get-tuple-element.34, f32[]{:T(128)S(6)} %rsqrt.75), kind=kLoop, calls=%fused_computation | loop fusion | flops 7340032 | bytes 22020100 | tf_op jit(solution)/shard_map/convert_element_type | solution.py:98
  852.5 16.9 %reshape.110 = bf16[512,2,3584]{2,1,0:T(2,128)(2,1)} reshape(bf16[512,7168]{1,0:T(8,128)(2,1)} %multiply_convert_fusion) | data formatting | bytes 14680064 | tf_op jit(solution)/shard_map/reshape | solution.py:99
  (77 shorter events, 38.6 us)
Async XLA Ops:
  7.2 89.3 %all-gather.3.cloned.1.call-start = ((), (), s32[]{:S(2)}) async-start(), calls=%async_computation | async-start | bytes 88080384 | tf_op jit(solution)/shard_map/all_gather | solution.py:41
  7.9 4.6 copy-start.1
  7.9 4.6 copy-start.2
  7.9 214.9 %all-reduce.7.cloned.1.call-start = ((), (), s32[]{:S(2)}) async-start(), calls=%async_computation.1 | async-start | bytes 1048576 | tf_op jit(solution)/shard_map/psum | solution.py:63
  96.4 39.3 %copy-start.4 = (f32[4096]{0:T(1024)S(1)}, f32[4096]{0:T(1024)}, u32[]{:S(2)}) copy-start(f32[4096]{0:T(1024)} %param.9) | copy-start | bytes 49156
  183.2 43.0 %copy-start.6 = (f32[3]{0:T(128)S(1)}, f32[3]{0:T(128)}, u32[]{:S(2)}) copy-start(f32[3]{0:T(128)} %param.13) | copy-start | bytes 40
  183.3 97.6 %all-reduce.9.cloned.1.call-start = ((), (), s32[]{:S(2)}) async-start(), calls=%async_computation.2 | async-start | bytes 1048576 | tf_op jit(solution)/shard_map/psum | solution.py:64
  226.2 143.1 %all-reduce.11.cloned.1.call-start = ((), (), s32[]{:S(2)}) async-start(), calls=%async_computation.3 | async-start | bytes 1048576 | tf_op jit(solution)/shard_map/psum | solution.py:63
  331.5 96.9 %copy-start.3 = (f32[32,4096]{1,0:T(8,128)S(1)}, f32[32,4096]{1,0:T(8,128)}, u32[]{:S(2)}) copy-start(f32[32,4096]{1,0:T(8,128)} %all-reduce.9.cloned.1.call-done) | copy-start | bytes 1572868
  331.6 95.7 %all-reduce.13.cloned.1.call-start = ((), (), s32[]{:S(2)}) async-start(), calls=%async_computation.4 | async-start | bytes 1048576 | tf_op jit(solution)/shard_map/psum | solution.py:64
  372.6 143.8 %all-reduce.15.cloned.1.call-start = ((), (), s32[]{:S(2)}) async-start(), calls=%async_computation.5 | async-start | bytes 1048576 | tf_op jit(solution)/shard_map/psum | solution.py:63
  478.6 95.8 %all-reduce.17.cloned.1.call-start = ((), (), s32[]{:S(2)}) async-start(), calls=%async_computation.6 | async-start | bytes 1048576 | tf_op jit(solution)/shard_map/psum | solution.py:64
  519.7 256.3 %all-gather.5.cloned.1.call-start = ((), (), s32[]{:S(2)}) async-start(), calls=%async_computation.7 | async-start | bytes 33030144 | tf_op jit(solution)/shard_map/all_gather | solution.py:93
  581.1 3.4 copy-start
  619.1 1.3 copy-start.5
  620.4 5.1 collective-permute-start
  620.4 9.3 %collective-permute-start.1 = (bf16[256,512]{1,0:T(8,128)(2,1)}, bf16[256,512]{1,0:T(8,128)(2,1)S(1)}, u32[]{:S(2)}, u32[]{:S(2)}) collective-permute-start(bf16[256,512]{1,0:T(8,128)(2,1)} %get-tuple-element.21), channel_id=1, source_target_pairs={{0,2},{1,3},{2,0},{3,1},{4,6},{5,7},{6,4},{7,5},{8,10},{9,11},{10,... | collective-permute-start | bytes 786440 | tf_op jit(solution)/shard_map/ppermute | solution.py:87
  621.2 17.2 %collective-permute-start.2 = (bf16[256,512]{1,0:T(8,128)(2,1)S(1)}, bf16[256,512]{1,0:T(8,128)(2,1)S(1)}, u32[]{:S(2)}, u32[]{:S(2)}) collective-permute-start(bf16[256,512]{1,0:T(8,128)(2,1)S(1)} %get-tuple-element.20), channel_id=1, source_target_pairs={{0,3},{1,2},{2,1},{3,0},{4,7},{5,6},{6,5},{7,4},{8,11},{9,10},{10,... | collective-permute-start | bytes 786440 | tf_op jit(solution)/shard_map/ppermute | solution.py:87
  622.3 16.9 %collective-permute-start.3 = (bf16[256,512]{1,0:T(8,128)(2,1)S(1)}, bf16[256,512]{1,0:T(8,128)(2,1)S(1)}, u32[]{:S(2)}, u32[]{:S(2)}) collective-permute-start(bf16[256,512]{1,0:T(8,128)(2,1)S(1)} %get-tuple-element.19), channel_id=1, source_target_pairs={{0,4},{1,5},{2,6},{3,7},{4,0},{5,1},{6,2},{7,3},{8,12},{9,13},{10,... | collective-permute-start | bytes 786440 | tf_op jit(solution)/shard_map/ppermute | solution.py:87
  623.0 19.5 %collective-permute-start.4 = (bf16[256,512]{1,0:T(8,128)(2,1)S(1)}, bf16[256,512]{1,0:T(8,128)(2,1)S(1)}, u32[]{:S(2)}, u32[]{:S(2)}) collective-permute-start(bf16[256,512]{1,0:T(8,128)(2,1)S(1)} %get-tuple-element.18), channel_id=1, source_target_pairs={{0,5},{1,4},{2,7},{3,6},{4,1},{5,0},{6,3},{7,2},{8,13},{9,12},{10,... | collective-permute-start | bytes 786440 | tf_op jit(solution)/shard_map/ppermute | solution.py:87
  625.5 24.8 %collective-permute-start.5 = (bf16[256,512]{1,0:T(8,128)(2,1)S(1)}, bf16[256,512]{1,0:T(8,128)(2,1)S(1)}, u32[]{:S(2)}, u32[]{:S(2)}) collective-permute-start(bf16[256,512]{1,0:T(8,128)(2,1)S(1)} %get-tuple-element.17), channel_id=1, source_target_pairs={{0,6},{1,7},{2,4},{3,5},{4,2},{5,3},{6,0},{7,1},{8,14},{9,15},{10,... | collective-permute-start | bytes 786440 | tf_op jit(solution)/shard_map/ppermute | solution.py:87
  629.7 30.8 %collective-permute-start.6 = (bf16[256,512]{1,0:T(8,128)(2,1)S(1)}, bf16[256,512]{1,0:T(8,128)(2,1)S(1)}, u32[]{:S(2)}, u32[]{:S(2)}) collective-permute-start(bf16[256,512]{1,0:T(8,128)(2,1)S(1)} %get-tuple-element.16), channel_id=1, source_target_pairs={{0,7},{1,6},{2,5},{3,4},{4,3},{5,2},{6,1},{7,0},{8,15},{9,14},{10,... | collective-permute-start | bytes 786440 | tf_op jit(solution)/shard_map/ppermute | solution.py:87
Sparse Core Ops, SparseCore 0:
  9.5 86.8 all-gather.2
  183.4 39.4 all-reduce.6
  226.3 54.5 all-reduce.8
  331.7 37.5 all-reduce.10
  372.7 54.5 all-reduce.12
  478.7 37.5 all-reduce.14
  519.8 54.5 all-reduce.16
  618.0 157.9 all-gather.4
